TPU v7x, 256 devices: a whole 4x4x8 slice. The times are simulated.
256 devices in a mesh: row: 16 (over z, core), col: 8 (over x, y_lo), vec: 2 (over y_hi).
Axes of the slice: x: 4, y: 4 (y_hi: 2, y_lo: 2; y = y_hi * 2 + y_lo), z: 8, core: 2. Of those that a mesh axis runs over, the one named last changes fastest.
Arguments:
- vectors: bfloat16 [16, 131072], P('vec', ('row', 'col')), may hold values from -6 to 6
- tile_vals: bfloat16 [16, 8, 256, 128, 128], P('row', 'col'), may hold values from -0.09375 to 0.09375
- tile_rows: int32 [16, 8, 256], P('row', 'col'), may hold values from 0 to 1023, as said below
- tile_cols: int32 [16, 8, 256], P('row', 'col'), may hold values from 0 to 1023, as said below
- tile_counts: int32 [16, 8], P('row', 'col'), may hold values from 1 to 256, as said below
Outputs:
- product: bfloat16 [16, 131072], P('vec', ('row', 'col'))
- gram: float32 [16, 16], P(None, 'vec')
Inputs may be any that keep to these rules, and one draw needn't show every extreme that they name: `tile_rows`: list [i, j] names tiles whose row index r has i * 64 <= r < (i + 1) * 64 and whose column index c has (c // 8) % (8) == j, that is the column's block of 8 tile rows, numbered c // 8, is held by column group j; live slots name distinct tiles with r >= c; slots at or beyond the count hold in-range indices that must be ignored. `tile_cols`: see tile_rows; the same slots. `tile_counts`: some lists are full in every draw; lists near the top of the triangle hold few tiles.
All inputs are finite; a program needn't handle non-finite values.
Results may differ from a plain program's by a relative error of at most 0.001.
Values may be sent and summed in bfloat16 or wider, within the bound.
A program may use at most 64 MiB of HBM per device.

v0:
```python
import math
import jax
import jax.numpy as jnp
from jax import lax
from jax.sharding import PartitionSpec as P


def shards(vectors, tile_vals, tile_rows, tile_cols, tile_counts):
    nrow = lax.axis_size("row")
    ncol = lax.axis_size("col")
    vlocal, width = vectors.shape
    tile = tile_vals.shape[-1]
    stretch = width // tile
    span = ncol * stretch
    colspan = nrow * stretch
    row_x = lax.all_gather(vectors, "col", axis=1, tiled=True)
    col_x = lax.all_gather(vectors, "row", axis=1, tiled=True)
    tiles = tile_vals[0, 0]
    rows = tile_rows[0, 0]
    cols = tile_cols[0, 0]
    count = tile_counts[0, 0]
    slots = jnp.arange(rows.shape[0], dtype=jnp.int32)
    live = slots < count
    mirror = live & (rows != cols)
    row_place = rows % span
    col_place = cols // span * stretch + cols % stretch
    row_blocks = row_x.reshape(vlocal, span, tile)
    col_blocks = col_x.reshape(vlocal, colspan, tile)
    picked_cols = jnp.take(col_blocks, col_place, axis=1)
    picked_rows = jnp.take(row_blocks, row_place, axis=1)
    down = jnp.einsum("tij,vtj->vti", tiles, picked_cols, preferred_element_type=jnp.float32)
    upper = jnp.einsum("tij,vti->vtj", tiles, picked_rows, preferred_element_type=jnp.float32)
    row_hit = (
        (row_place[None, :] == jnp.arange(span, dtype=jnp.int32)[:, None]) & live[None, :]
    ).astype(jnp.float32)
    col_hit = (
        (col_place[None, :] == jnp.arange(colspan, dtype=jnp.int32)[:, None]) & mirror[None, :]
    ).astype(jnp.float32)
    row_part = jnp.einsum("at,vti->vai", row_hit, down, precision=lax.Precision.HIGHEST).reshape(
        vlocal, span * tile
    )
    col_part = jnp.einsum("at,vti->vai", col_hit, upper, precision=lax.Precision.HIGHEST).reshape(
        vlocal, colspan * tile
    )
    row_whole = lax.psum(row_part, "col")
    col_whole = lax.psum(col_part, "row")
    row_share = lax.dynamic_slice_in_dim(row_whole, lax.axis_index("col") * width, width, 1)
    col_share = lax.dynamic_slice_in_dim(col_whole, lax.axis_index("row") * width, width, 1)
    image = row_share + col_share
    every_vector = lax.all_gather(vectors, "vec", axis=0, tiled=True)
    partial_gram = jnp.dot(
        every_vector.astype(jnp.float32), image.T, precision=lax.Precision.HIGHEST
    )
    gram = lax.psum(partial_gram, ("row", "col")) / math.sqrt(width * nrow * ncol)
    return (image.astype(jnp.bfloat16), gram)


def solution(mesh):
    return jax.shard_map(
        shards,
        mesh=mesh,
        in_specs=(
            P("vec", ("row", "col")),
            P("row", "col", None, None, None),
            P("row", "col", None),
            P("row", "col", None),
            P("row", "col"),
        ),
        out_specs=(P("vec", ("row", "col")), P(None, "vec")),
        check_vma=False,
    )
```

profile of v0, /device:TPU:8, one launch (start us, length us, event | category | flops | bytes accessed | tf_op | source)
XLA Modules:
  0.0 527.4 jit_solution(8425430569256399796)
XLA Ops:
  7.2 0.0 copy-start.1
  7.2 0.0 copy-start.2
  7.2 0.0 all-reduce.5.cloned.1.call-start
  7.2 28.5 %all_gather.10 = bf16[8,8192]{1,0:T(8,128)(2,1)S(1)} all-gather(bf16[8,1024]{1,0:T(8,128)(2,1)} %param.5), channel_id=1, replica_groups=mesh['row'=16,'col'=8,'vec'=2] {'col'}, dimensions={1}, use_global_device_ids=true | all-gather | bytes 147456 | tf_op jit(solution)/shard_map/all_gather | solution.py:16
  35.8 0.7 compare_select_fusion
  36.5 0.7 compare_and_fusion.1
  37.2 0.8 gather_fusion.1
  38.0 0.0 copy-start
  38.0 4.7 fusion
  42.7 0.4 copy.9
  43.8 0.0 copy-done.1
  43.8 0.0 copy-done.2
  43.8 0.6 convolution_bitcast_fusion
  44.5 0.2 copy.7
  44.7 1.1 copy.18
  45.8 0.0 all-reduce.5.cloned.1.call-update
  45.8 0.0 all-reduce.3.cloned.1.call-start
  45.9 0.0 copy-done
  45.9 20.7 %all_gather.9 = bf16[8,16384]{1,0:T(8,128)(2,1)S(1)} all-gather(bf16[8,1024]{1,0:T(8,128)(2,1)S(1)} %copy-done), channel_id=1, replica_groups=mesh['row'=16,'col'=8,'vec'=2] {'row'}, dimensions={1}, use_global_device_ids=true | all-gather | bytes 278528 | tf_op jit(solution)/shard_map/all_gather | solution.py:17
  66.6 0.8 gather_fusion
  67.4 6.8 %fusion.2 = f32[256,8,128]{2,1,0:T(8,128)S(1)} fusion(bf16[1,1,256,128,128]{4,3,2,1,0:T(8,128)(2,1)} %param.6, bf16[256,8,128]{2,1,0:T(8,128)(2,1)S(1)} %gather_fusion, pred[256]{0:T(512)(128)(4,1)S(1)} %get-tuple-element.2), kind=kOutput, calls=%fused_computation.4 | convolution fusion | flops 67371008 | bytes 9961728 | tf_op jit(solution)/shard_map/tij,vtj->vti/dot_general | solution.py:31
  74.2 0.6 convolution_bitcast_fusion.1
  74.8 0.9 copy.19
  75.7 0.0 all-reduce.3.cloned.1.call-update
  75.7 5.9 %all_gather.11 = bf16[16,1024]{1,0:T(8,128)(2,1)S(1)} all-gather(bf16[8,1024]{1,0:T(8,128)(2,1)S(1)} %copy-done), channel_id=1, replica_groups=mesh['row'=16,'col'=8,'vec'=2] {'vec'}, dimensions={0}, use_global_device_ids=true | all-gather | bytes 49152 | tf_op jit(solution)/shard_map/all_gather | solution.py:50
  81.7 77.3 %all-reduce.5.cloned.1.call-done = f32[8,16384]{1,0:T(8,128)} async-done(((f32[8,16384]{1,0:T(8,128)}), f32[8,16384]{1,0:T(8,128)}) %all-reduce.5.cloned.1.call-update) | async-done | bytes 524304 | tf_op jit(solution)/shard_map/psum | solution.py:46
  159.0 79.9 %all-reduce.3.cloned.1.call-done = f32[8,8192]{1,0:T(8,128)} async-done(((f32[8,8192]{1,0:T(8,128)}), f32[8,8192]{1,0:T(8,128)}) %all-reduce.3.cloned.1.call-update) | async-done | bytes 262160 | tf_op jit(solution)/shard_map/psum | solution.py:45
  238.9 0.9 convolution_bitcast_fusion.2
  239.8 278.8 %psum.23 = f32[16,8]{0,1:T(8,128)S(1)} all-reduce(f32[16,8]{0,1:T(8,128)S(1)} %convolution_bitcast_fusion.2), channel_id=1, replica_groups=mesh['row'=16,'col'=8,'vec'=2] {'row','col'}, use_global_device_ids=true, to_apply=%region_2.3 | all-reduce | flops 128 | bytes 1024 | tf_op jit(solution)/shard_map/psum | solution.py:54
  518.6 0.6 broadcast_multiply_fusion
  519.2 1.4 fusion.25
  (5 shorter events, 0.1 us)
Async XLA Ops:
  7.2 36.6 %copy-start.1 = (s32[1,1,256]{2,1,0:T(1,128)S(1)}, s32[1,1,256]{2,1,0:T(1,128)}, u32[]{:S(2)}) copy-start(s32[1,1,256]{2,1,0:T(1,128)} %param.7) | copy-start | bytes 3076
  7.2 36.6 %copy-start.2 = (s32[1,1,256]{2,1,0:T(1,128)S(1)}, s32[1,1,256]{2,1,0:T(1,128)}, u32[]{:S(2)}) copy-start(s32[1,1,256]{2,1,0:T(1,128)} %param.8) | copy-start | bytes 3076
  7.2 151.8 %all-reduce.5.cloned.1.call-start = ((), (), s32[]{:S(2)}) async-start(), calls=%async_computation.1 | async-start | bytes 1048576 | tf_op jit(solution)/shard_map/psum | solution.py:46
  38.0 7.9 %copy-start = (bf16[8,1024]{1,0:T(8,128)(2,1)S(1)}, bf16[8,1024]{1,0:T(8,128)(2,1)}, u32[]{:S(2)}) copy-start(bf16[8,1024]{1,0:T(8,128)(2,1)} %param.5) | copy-start | bytes 49156
  45.8 193.1 %all-reduce.3.cloned.1.call-start = ((), (), s32[]{:S(2)}) async-start(), calls=%async_computation | async-start | bytes 524288 | tf_op jit(solution)/shard_map/psum | solution.py:45
Sparse Core Ops, SparseCore 0:
  45.9 113.0 all-reduce.4
  161.6 77.2 all-reduce.2
where the time goes:
time: 528 us; the launch traced here: 527 us
  blocking collectives  334 us (63%)
  waiting for transfers between devices  157 us (30%)
  between operations  14.8 us (3%)
  matrix products  13.7 us (3%)
    psum x1, blocking collectives, shards(): lax.psum(partial_gram, ('row', 'col')) / math.sqrt(width * nrow * ncol)  279 us
    psum x1, waiting for transfers between devices, shards(): row_whole = lax.psum(row_part, 'col')  79.9 us
    psum x1, waiting for transfers between devices, shards(): col_whole = lax.psum(col_part, 'row')  77.3 us
    all_gather x1, blocking collectives, shards(): row_x = lax.all_gather(vectors, 'col', axis=1, tiled=True)  28.5 us
    all_gather x1, blocking collectives, shards(): col_x = lax.all_gather(vectors, 'row', axis=1, tiled=True)  20.7 us
  transfers between devices with their start and end apart: 2, of which 2 were waited for; matrix products, arithmetic and copies ran while one was open for 2% of the time, Pallas kernels for 0%

commit v1 on v0

--- a/solution.py
+++ b/solution.py
@@ -51,7 +51,7 @@
     partial_gram = jnp.dot(
         every_vector.astype(jnp.float32), image.T, precision=lax.Precision.HIGHEST
     )
-    gram = lax.psum(partial_gram, ("row", "col")) / math.sqrt(width * nrow * ncol)
+    gram = lax.psum(lax.psum(partial_gram, "col"), "row") / math.sqrt(width * nrow * ncol)
     return (image.astype(jnp.bfloat16), gram)
 
 

time: 528 us -> 294 us (0.56)
  blocking collectives: 334 us -> 97.5 us
    psum x1 -> x2, blocking collectives: 279 us -> 42.4 us  [the longest x1 23.5 us: shards(): lax.psum(lax.psum(partial_gram, 'col'), 'row')]
  transfers between devices with their start and end apart: 2 -> 2, of which waited for: 2 -> 2; matrix products, arithmetic and copies ran while one was open for 2% -> 3% of each run, Pallas kernels for 0% -> 0%
where the time goes in v1:
time: 294 us; the launch traced here: 291 us
  waiting for transfers between devices  157 us (53%)
  blocking collectives  97.5 us (33%)
  between operations  14.8 us (5%)
  matrix products  13.7 us (5%)
  local copies, waits for them, and re-layouts  4.24 us (1%)
  other arithmetic  3.42 us (1%)
    psum x1, waiting for transfers between devices, shards(): row_whole = lax.psum(row_part, 'col')  79.9 us
    psum x1, waiting for transfers between devices, shards(): col_whole = lax.psum(col_part, 'row')  77.3 us
    all_gather x1, blocking collectives, shards(): row_x = lax.all_gather(vectors, 'col', axis=1, tiled=True)  28.5 us
    psum x1, blocking collectives, shards(): lax.psum(lax.psum(partial_gram, 'col'), 'row')  23.5 us
    all_gather x1, blocking collectives, shards(): col_x = lax.all_gather(vectors, 'row', axis=1, tiled=True)  20.7 us
    psum x1, blocking collectives, shards(): lax.psum(partial_gram, 'col')  18.9 us
    dot_general x1, matrix products, shards(): jnp.einsum('tij,vtj->vti', tiles, picked_cols, preferred_element_type=jnp...  6.82 us
    all_gather x1, blocking collectives, shards(): every_vector = lax.all_gather(vectors, 'vec', axis=0, tiled=True)  5.91 us
  transfers between devices with their start and end apart: 2, of which 2 were waited for; matrix products, arithmetic and copies ran while one was open for 3% of the time, Pallas kernels for 0%

profile of v1, /device:TPU:8, one launch (start us, length us, event | category | flops | bytes accessed | tf_op | source)
XLA Modules:
  0.0 291.0 jit_solution(14123897199318023767)
XLA Ops:
  7.2 0.0 copy-start.1
  7.2 0.0 copy-start.2
  7.2 0.0 all-reduce.5.cloned.1.call-start
  7.2 28.5 %all_gather.10 = bf16[8,8192]{1,0:T(8,128)(2,1)S(1)} all-gather(bf16[8,1024]{1,0:T(8,128)(2,1)} %param.5), channel_id=1, replica_groups=mesh['row'=16,'col'=8,'vec'=2] {'col'}, dimensions={1}, use_global_device_ids=true | all-gather | bytes 147456 | tf_op jit(solution)/shard_map/all_gather | solution.py:16
  35.8 0.7 compare_select_fusion
  36.5 0.7 compare_and_fusion.1
  37.2 0.8 gather_fusion.1
  38.0 0.0 copy-start
  38.0 4.7 %fusion = f32[256,8,128]{2,1,0:T(8,128)S(1)} fusion(bf16[1,1,256,128,128]{4,3,2,1,0:T(8,128)(2,1)} %param.6, bf16[256,8,128]{2,1,0:T(8,128)(2,1)S(1)} %gather_fusion.1, pred[256]{0:T(512)(128)(4,1)S(1)} %get-tuple-element.4), kind=kOutput, calls=%fused_computation.2 | convolution fusion | flops 67371008 | bytes 9961728 | tf_op jit(solution)/shard_map/tij,vti->vtj/dot_general | solution.py:32
  42.7 0.4 copy.9
  43.8 0.0 copy-done.1
  43.8 0.0 copy-done.2
  43.8 0.6 convolution_bitcast_fusion
  44.5 0.2 copy.7
  44.7 1.1 copy.18
  45.8 0.0 all-reduce.5.cloned.1.call-update
  45.8 0.0 all-reduce.3.cloned.1.call-start
  45.9 0.0 copy-done
  45.9 20.7 %all_gather.9 = bf16[8,16384]{1,0:T(8,128)(2,1)S(1)} all-gather(bf16[8,1024]{1,0:T(8,128)(2,1)S(1)} %copy-done), channel_id=1, replica_groups=mesh['row'=16,'col'=8,'vec'=2] {'row'}, dimensions={1}, use_global_device_ids=true | all-gather | bytes 278528 | tf_op jit(solution)/shard_map/all_gather | solution.py:17
  66.6 0.8 gather_fusion
  67.4 6.8 %fusion.2 = f32[256,8,128]{2,1,0:T(8,128)S(1)} fusion(bf16[1,1,256,128,128]{4,3,2,1,0:T(8,128)(2,1)} %param.6, bf16[256,8,128]{2,1,0:T(8,128)(2,1)S(1)} %gather_fusion, pred[256]{0:T(512)(128)(4,1)S(1)} %get-tuple-element.2), kind=kOutput, calls=%fused_computation.4 | convolution fusion | flops 67371008 | bytes 9961728 | tf_op jit(solution)/shard_map/tij,vtj->vti/dot_general | solution.py:31
  74.2 0.6 convolution_bitcast_fusion.1
  74.9 0.9 copy.19
  75.7 0.0 all-reduce.3.cloned.1.call-update
  75.8 5.9 %all_gather.11 = bf16[16,1024]{1,0:T(8,128)(2,1)S(1)} all-gather(bf16[8,1024]{1,0:T(8,128)(2,1)S(1)} %copy-done), channel_id=1, replica_groups=mesh['row'=16,'col'=8,'vec'=2] {'vec'}, dimensions={0}, use_global_device_ids=true | all-gather | bytes 49152 | tf_op jit(solution)/shard_map/all_gather | solution.py:50
  81.7 77.3 %all-reduce.5.cloned.1.call-done = f32[8,16384]{1,0:T(8,128)} async-done(((f32[8,16384]{1,0:T(8,128)}), f32[8,16384]{1,0:T(8,128)}) %all-reduce.5.cloned.1.call-update) | async-done | bytes 524304 | tf_op jit(solution)/shard_map/psum | solution.py:46
  159.0 79.9 %all-reduce.3.cloned.1.call-done = f32[8,8192]{1,0:T(8,128)} async-done(((f32[8,8192]{1,0:T(8,128)}), f32[8,8192]{1,0:T(8,128)}) %all-reduce.3.cloned.1.call-update) | async-done | bytes 262160 | tf_op jit(solution)/shard_map/psum | solution.py:45
  238.9 0.9 convolution_bitcast_fusion.2
  239.8 18.9 %psum.30 = f32[16,8]{0,1:T(8,128)S(1)} all-reduce(f32[16,8]{0,1:T(8,128)S(1)} %convolution_bitcast_fusion.2), channel_id=1, replica_groups=mesh['row'=16,'col'=8,'vec'=2] {'col'}, use_global_device_ids=true, to_apply=%region_2.3 | all-reduce | flops 128 | bytes 1024 | tf_op jit(solution)/shard_map/psum | solution.py:54
  258.7 23.5 %psum.31 = f32[16,8]{0,1:T(8,128)S(1)} all-reduce(f32[16,8]{0,1:T(8,128)S(1)} %psum.30), channel_id=1, replica_groups=mesh['row'=16,'col'=8,'vec'=2] {'row'}, use_global_device_ids=true, to_apply=%region_3.4 | all-reduce | flops 128 | bytes 1024 | tf_op jit(solution)/shard_map/psum | solution.py:54
  282.2 0.6 broadcast_multiply_fusion
  282.8 1.4 fusion.25
  (5 shorter events, 0.1 us)
Async XLA Ops:
  7.2 36.6 %copy-start.1 = (s32[1,1,256]{2,1,0:T(1,128)S(1)}, s32[1,1,256]{2,1,0:T(1,128)}, u32[]{:S(2)}) copy-start(s32[1,1,256]{2,1,0:T(1,128)} %param.7) | copy-start | bytes 3076
  7.2 36.6 %copy-start.2 = (s32[1,1,256]{2,1,0:T(1,128)S(1)}, s32[1,1,256]{2,1,0:T(1,128)}, u32[]{:S(2)}) copy-start(s32[1,1,256]{2,1,0:T(1,128)} %param.8) | copy-start | bytes 3076
  7.2 151.8 %all-reduce.5.cloned.1.call-start = ((), (), s32[]{:S(2)}) async-start(), calls=%async_computation.1 | async-start | bytes 1048576 | tf_op jit(solution)/shard_map/psum | solution.py:46
  38.0 7.9 %copy-start = (bf16[8,1024]{1,0:T(8,128)(2,1)S(1)}, bf16[8,1024]{1,0:T(8,128)(2,1)}, u32[]{:S(2)}) copy-start(bf16[8,1024]{1,0:T(8,128)(2,1)} %param.5) | copy-start | bytes 49156
  45.8 193.1 %all-reduce.3.cloned.1.call-start = ((), (), s32[]{:S(2)}) async-start(), calls=%async_computation | async-start | bytes 524288 | tf_op jit(solution)/shard_map/psum | solution.py:45
Sparse Core Ops, SparseCore 0:
  45.9 113.0 all-reduce.4
  161.6 77.2 all-reduce.2

commit v2 on v0

--- a/solution.py
+++ b/solution.py
@@ -43,7 +43,11 @@
         vlocal, colspan * tile
     )
     row_whole = lax.psum(row_part, "col")
-    col_whole = lax.psum(col_part, "row")
+    col_whole = col_part
+    for hop in (1, 2, 4, 8):
+        col_whole = col_whole + lax.ppermute(
+            col_whole, "row", [(dev, dev ^ hop) for dev in range(16)]
+        )
     row_share = lax.dynamic_slice_in_dim(row_whole, lax.axis_index("col") * width, width, 1)
     col_share = lax.dynamic_slice_in_dim(col_whole, lax.axis_index("row") * width, width, 1)
     image = row_share + col_share

time: 528 us -> 471 us (0.89)
  waiting for transfers between devices: 157 us -> 89.4 us
  blocking collectives: 334 us -> 341 us
  starting transfers between devices: 0.08 us -> 5.68 us
    psum x1 -> x0, waiting for transfers between devices: 77.3 us -> none  [shards(): col_whole = lax.psum(col_part, 'row')]
    ppermute x0 -> x4, waiting for transfers between devices: none -> 20.4 us  [shards(): lax.ppermute(col_whole, 'row', [(dev, dev ^ hop) for dev in range(16)])]
    psum x1, waiting for transfers between devices: 79.9 us -> 69 us  [shards(): row_whole = lax.psum(row_part, 'col')]
    all_gather x1, blocking collectives: 20.7 us -> 27.5 us  [shards(): col_x = lax.all_gather(vectors, 'row', axis=1, tiled=True)]
    ppermute x0 -> x4, starting transfers between devices: none -> 5.65 us  [shards(): lax.ppermute(col_whole, 'row', [(dev, dev ^ hop) for dev in range(16)])]
  transfers between devices with their start and end apart: 2 -> 5, of which waited for: 2 -> 3; matrix products, arithmetic and copies ran while one was open for 2% -> 2% of each run, Pallas kernels for 0% -> 0%
where the time goes in v2:
time: 471 us
  blocking collectives  341 us (72%)
  waiting for transfers between devices  89.4 us (19%)
  between operations  14.8 us (3%)
  matrix products  12.9 us (3%)
  starting transfers between devices  5.68 us (1%)
    psum x1, blocking collectives, shards(): lax.psum(partial_gram, ('row', 'col')) / math.sqrt(width * nrow * ncol)  279 us
    psum x1, waiting for transfers between devices, shards(): row_whole = lax.psum(row_part, 'col')  69 us
    all_gather x1, blocking collectives, shards(): row_x = lax.all_gather(vectors, 'col', axis=1, tiled=True)  28.5 us
    all_gather x1, blocking collectives, shards(): col_x = lax.all_gather(vectors, 'row', axis=1, tiled=True)  27.5 us
    ppermute x4, waiting for transfers between devices, shards(): lax.ppermute(col_whole, 'row', [(dev, dev ^ hop) for dev in range(16)])  20.4 us
  transfers between devices with their start and end apart: 5, of which 3 were waited for; matrix products, arithmetic and copies ran while one was open for 2% of the time, Pallas kernels for 0%

profile of v2, /device:TPU:8, one launch (start us, length us, event | category | flops | bytes accessed | tf_op | source)
XLA Modules:
  0.0 470.8 jit_solution(1012153885541332367)
XLA Ops:
  7.2 0.0 copy-start.1
  7.2 0.0 copy-start.2
  7.2 0.0 all-reduce.2.cloned.1.call-start
  7.9 0.7 compare_and_fusion.1
  8.6 0.7 compare_select_fusion
  9.3 28.5 %all_gather.10 = bf16[8,8192]{1,0:T(8,128)(2,1)S(1)} all-gather(bf16[8,1024]{1,0:T(8,128)(2,1)} %param.5), channel_id=1, replica_groups=mesh['row'=16,'col'=8,'vec'=2] {'col'}, dimensions={1}, use_global_device_ids=true | all-gather | bytes 147456 | tf_op jit(solution)/shard_map/all_gather | solution.py:16
  37.9 0.8 gather_fusion.1
  38.7 0.0 copy-start
  38.7 4.7 %fusion = f32[256,8,128]{2,1,0:T(8,128)S(1)} fusion(bf16[1,1,256,128,128]{4,3,2,1,0:T(8,128)(2,1)} %param.6, bf16[256,8,128]{2,1,0:T(8,128)(2,1)S(1)} %gather_fusion.1, pred[256]{0:T(512)(128)(4,1)S(1)} %get-tuple-element.6), kind=kOutput, calls=%fused_computation.2 | convolution fusion | flops 67371008 | bytes 9961728 | tf_op jit(solution)/shard_map/tij,vti->vtj/dot_general | solution.py:32
  43.4 0.4 copy.9
  43.8 0.0 copy-done.1
  43.8 0.0 copy-done.2
  43.9 0.6 convolution_bitcast_fusion
  44.5 0.2 copy.7
  44.7 0.3 copy.20
  45.0 0.1 collective-permute-start
  45.1 1.9 collective-permute-done
  47.0 0.3 fusion.32
  47.4 2.0 collective-permute-start.1
  49.4 0.0 copy-done
  49.4 27.5 %all_gather.9 = bf16[8,16384]{1,0:T(8,128)(2,1)S(1)} all-gather(bf16[8,1024]{1,0:T(8,128)(2,1)S(1)} %copy-done), channel_id=1, replica_groups=mesh['row'=16,'col'=8,'vec'=2] {'row'}, dimensions={1}, use_global_device_ids=true | all-gather | bytes 278528 | tf_op jit(solution)/shard_map/all_gather | solution.py:17
  76.8 0.8 gather_fusion
  77.7 0.0 collective-permute-done.1
  77.7 0.1 add.149
  77.7 0.3 collective-permute-start.2
  78.1 6.8 %fusion.2 = f32[256,8,128]{2,1,0:T(8,128)S(1)} fusion(bf16[1,1,256,128,128]{4,3,2,1,0:T(8,128)(2,1)} %param.6, bf16[256,8,128]{2,1,0:T(8,128)(2,1)S(1)} %gather_fusion, pred[256]{0:T(512)(128)(4,1)S(1)} %get-tuple-element.4), kind=kOutput, calls=%fused_computation.4 | convolution fusion | flops 67371008 | bytes 9961728 | tf_op jit(solution)/shard_map/tij,vtj->vti/dot_general | solution.py:31
  84.9 18.5 %collective-permute-done.2 = f32[8,16384]{1,0:T(8,128)S(1)} collective-permute-done((f32[8,16384]{1,0:T(8,128)S(1)}, f32[8,16384]{1,0:T(8,128)S(1)}, u32[]{:S(2)}, u32[]{:S(2)}) %collective-permute-start.2) | collective-permute-done | bytes 524320 | tf_op jit(solution)/shard_map/ppermute | solution.py:48
  103.4 0.1 add.150
  103.4 3.2 collective-permute-start.3
  106.6 0.6 convolution_bitcast_fusion.1
  107.2 0.9 copy.21
  108.1 0.0 all-reduce.2.cloned.1.call-update
  108.1 5.9 %all_gather.11 = bf16[16,1024]{1,0:T(8,128)(2,1)S(1)} all-gather(bf16[8,1024]{1,0:T(8,128)(2,1)S(1)} %copy-done), channel_id=1, replica_groups=mesh['row'=16,'col'=8,'vec'=2] {'vec'}, dimensions={0}, use_global_device_ids=true | all-gather | bytes 49152 | tf_op jit(solution)/shard_map/all_gather | solution.py:54
  114.1 69.0 %all-reduce.2.cloned.1.call-done = f32[8,8192]{1,0:T(8,128)} async-done(((f32[8,8192]{1,0:T(8,128)}), f32[8,8192]{1,0:T(8,128)}) %all-reduce.2.cloned.1.call-update) | async-done | bytes 262160 | tf_op jit(solution)/shard_map/psum | solution.py:45
  183.1 0.0 collective-permute-done.3
  183.1 1.4 fusion.33
  184.5 0.1 convolution_bitcast_fusion.2
  184.6 278.8 %psum.15 = f32[16,8]{0,1:T(8,128)S(1)} all-reduce(f32[16,8]{0,1:T(8,128)S(1)} %convolution_bitcast_fusion.2), channel_id=1, replica_groups=mesh['row'=16,'col'=8,'vec'=2] {'row','col'}, use_global_device_ids=true, to_apply=%region_1.2 | all-reduce | flops 128 | bytes 1024 | tf_op jit(solution)/shard_map/psum | solution.py:58
  463.4 0.6 broadcast_multiply_fusion
  (4 shorter events, 0.0 us)
Async XLA Ops:
  7.2 36.7 %copy-start.1 = (s32[1,1,256]{2,1,0:T(1,128)S(1)}, s32[1,1,256]{2,1,0:T(1,128)}, u32[]{:S(2)}) copy-start(s32[1,1,256]{2,1,0:T(1,128)} %param.7) | copy-start | bytes 3076
  7.2 36.7 %copy-start.2 = (s32[1,1,256]{2,1,0:T(1,128)S(1)}, s32[1,1,256]{2,1,0:T(1,128)}, u32[]{:S(2)}) copy-start(s32[1,1,256]{2,1,0:T(1,128)} %param.8) | copy-start | bytes 3076
  7.2 175.9 %all-reduce.2.cloned.1.call-start = ((), (), s32[]{:S(2)}) async-start(), calls=%async_computation | async-start | bytes 524288 | tf_op jit(solution)/shard_map/psum | solution.py:45
  38.7 10.7 %copy-start = (bf16[8,1024]{1,0:T(8,128)(2,1)S(1)}, bf16[8,1024]{1,0:T(8,128)(2,1)}, u32[]{:S(2)}) copy-start(bf16[8,1024]{1,0:T(8,128)(2,1)} %param.5) | copy-start | bytes 49156
  45.0 2.0 collective-permute-start
  47.4 30.3 %collective-permute-start.1 = (f32[8,16384]{1,0:T(8,128)S(1)}, f32[8,16384]{1,0:T(8,128)S(1)}, u32[]{:S(2)}, u32[]{:S(2)}) collective-permute-start(f32[8,16384]{1,0:T(8,128)S(1)} %fusion.32), channel_id=1, source_target_pairs={{0,32},{16,48},{32,0},{48,16},{64,96},{80,112},{96,64},{112,80},{1... | collective-permute-start | bytes 1572872 | tf_op jit(solution)/shard_map/ppermute | solution.py:48
  77.7 25.6 %collective-permute-start.2 = (f32[8,16384]{1,0:T(8,128)S(1)}, f32[8,16384]{1,0:T(8,128)S(1)}, u32[]{:S(2)}, u32[]{:S(2)}) collective-permute-start(f32[8,16384]{1,0:T(8,128)S(1)} %add.149), channel_id=1, source_target_pairs={{0,64},{16,80},{32,96},{48,112},{64,0},{80,16},{96,32},{112,48},{1... | collective-permute-start | bytes 1572872 | tf_op jit(solution)/shard_map/ppermute | solution.py:48
  103.4 79.7 %collective-permute-start.3 = (f32[8,16384]{1,0:T(8,128)S(1)}, f32[8,16384]{1,0:T(8,128)S(1)}, u32[]{:S(2)}, u32[]{:S(2)}) collective-permute-start(f32[8,16384]{1,0:T(8,128)S(1)} %add.150), channel_id=1, source_target_pairs={{0,128},{16,144},{32,160},{48,176},{64,192},{80,208},{96,224},{112... | collective-permute-start | bytes 1572872 | tf_op jit(solution)/shard_map/ppermute | solution.py:48
Sparse Core Ops, SparseCore 0:
  108.3 74.7 all-reduce.1
